TPU v7x, 256 devices: a whole 4x4x8 slice. The times are simulated.
256 devices in a mesh: seq: 32 (over x_hi, z, core), tp: 8 (over y, x_lo).
Axes of the slice: x: 4 (x_hi: 2, x_lo: 2; x = x_hi * 2 + x_lo), y: 4, z: 8, core: 2. Of those that a mesh axis runs over, the one named last changes fastest.
Arguments:
- queries: bfloat16 [8, 4096, 4096], P('tp', 'seq'), may hold values from -9 to 9
- key_rows: bfloat16 [8, 4096, 4096], P('tp', 'seq'), may hold values from -6 to 6
- values: bfloat16 [8, 4096, 4096], P('tp', 'seq'), may hold values from -6 to 6
- upstream: bfloat16 [8, 4096, 4096], P(None, 'seq', 'tp'), may hold values from -6 to 6
- out_weight: bfloat16 [4096, 4096], P(None, 'tp'), may hold values from -0.09375 to 0.09375
- blocks: int32 [64, 4], replicated, may hold values from 0 to 63, as said below
Outputs:
- attended: bfloat16 [8, 4096, 4096], P('tp', 'seq')
- grad_queries: bfloat16 [8, 4096, 4096], P('tp', 'seq')
- grad_keys: bfloat16 [8, 4096, 4096], P('tp', 'seq')
- grad_values: bfloat16 [8, 4096, 4096], P('tp', 'seq')
- grad_weight: float32 [4096, 4096], P('seq', 'tp')
Inputs may be any that keep to these rules, and one draw needn't show every extreme that they name: Row a lists the blocks a - 1, a and a + 1 modulo 64, then one block 2 to 62 blocks after a modulo 64; no row names a block twice.
All inputs are finite; a program needn't handle non-finite values.
Results may differ from a plain program's by a relative error of at most 0.022.
Values may be sent and summed in bfloat16 or wider, within the bound.
A program may use at most 128 MiB of HBM per device.

v0:
```python
import math
import jax
import jax.numpy as jnp
from jax import lax
from jax.sharding import PartitionSpec as P

HD = 128
BLK = 64
NB = 4


def forward_head(query_rows, key_rows, value_rows, blocks):
    block_count = blocks.shape[0]
    factor = 1.0 / math.sqrt(HD)
    query_tiles = query_rows.reshape(block_count, BLK, HD)
    key_set = key_rows.reshape(block_count, BLK, HD)[blocks].reshape(block_count, NB * BLK, HD)
    value_set = value_rows.reshape(block_count, BLK, HD)[blocks].reshape(block_count, NB * BLK, HD)
    scores = (
        jnp.einsum("qid,qjd->qij", query_tiles, key_set, preferred_element_type=jnp.float32)
        * factor
    )
    row_max = jnp.max(scores, axis=-1, keepdims=True)
    shifted = jnp.exp(scores - row_max)
    soft_probs = shifted / jnp.sum(shifted, axis=-1, keepdims=True)
    probs_low = soft_probs.astype(jnp.bfloat16)
    context = jnp.einsum(
        "qij,qjd->qid", probs_low, value_set, preferred_element_type=jnp.float32
    ).astype(jnp.bfloat16)
    return (context, soft_probs, probs_low, key_set, value_set)


def backward_head(query_rows, grad_rows, blocks, saved):
    context, soft_probs, probs_low, key_set, value_set = saved
    block_count = blocks.shape[0]
    factor = 1.0 / math.sqrt(HD)
    query_tiles = query_rows.reshape(block_count, BLK, HD)
    grad_tiles = grad_rows.reshape(block_count, BLK, HD)
    row_delta = jnp.sum(
        grad_tiles.astype(jnp.float32) * context.astype(jnp.float32), axis=-1, keepdims=True
    )
    dprobs = jnp.einsum("qid,qjd->qij", grad_tiles, value_set, preferred_element_type=jnp.float32)
    dscores = (soft_probs * (dprobs - row_delta) * factor).astype(jnp.bfloat16)
    query_grad = jnp.einsum(
        "qij,qjd->qid", dscores, key_set, preferred_element_type=jnp.float32
    ).astype(jnp.bfloat16)
    flat_list = blocks.reshape(-1)
    key_parts = jnp.einsum(
        "qij,qid->qjd", dscores, query_tiles, preferred_element_type=jnp.float32
    ).reshape(block_count * NB, BLK, HD)
    value_parts = jnp.einsum(
        "qij,qid->qjd", probs_low, grad_tiles, preferred_element_type=jnp.float32
    ).reshape(block_count * NB, BLK, HD)
    key_grad = (
        jnp.zeros((block_count, BLK, HD), jnp.float32)
        .at[flat_list]
        .add(key_parts)
        .astype(jnp.bfloat16)
    )
    value_grad = (
        jnp.zeros((block_count, BLK, HD), jnp.float32)
        .at[flat_list]
        .add(value_parts)
        .astype(jnp.bfloat16)
    )
    return (query_grad, key_grad, value_grad)


def on_device(queries, key_rows, values, upstream, out_weight, blocks):
    head_queries, head_keys, head_values = (
        lax.all_to_all(queries, "seq", split_axis=2, concat_axis=1, tiled=True),
        lax.all_to_all(key_rows, "seq", split_axis=2, concat_axis=1, tiled=True),
        lax.all_to_all(values, "seq", split_axis=2, concat_axis=1, tiled=True),
    )
    length = head_queries.shape[1]
    count_heads = head_queries.shape[2] // HD

    def split_heads(array):
        return array.reshape(length, count_heads, HD).transpose(1, 0, 2)

    def join_heads(array):
        return (
            array.reshape(count_heads, length, HD)
            .transpose(1, 0, 2)
            .reshape(1, length, count_heads * HD)
        )

    grad_tokens = lax.psum_scatter(
        jnp.einsum("stc,dc->std", upstream, out_weight, preferred_element_type=jnp.float32).astype(
            jnp.bfloat16
        ),
        "tp",
        scatter_dimension=0,
        tiled=True,
    )
    grad_heads = lax.all_to_all(grad_tokens, "seq", split_axis=2, concat_axis=1, tiled=True)
    stacked = (
        split_heads(head_queries),
        split_heads(head_keys),
        split_heads(head_values),
        split_heads(grad_heads),
    )

    def both_one(packed):
        saved_one = forward_head(packed[0], packed[1], packed[2], blocks)
        return (saved_one[0],) + backward_head(packed[0], packed[3], blocks, saved_one)

    results = lax.map(both_one, stacked)
    attended, query_grad, key_grad, value_grad = (
        lax.all_to_all(join_heads(results[0]), "seq", split_axis=1, concat_axis=2, tiled=True),
        lax.all_to_all(join_heads(results[1]), "seq", split_axis=1, concat_axis=2, tiled=True),
        lax.all_to_all(join_heads(results[2]), "seq", split_axis=1, concat_axis=2, tiled=True),
        lax.all_to_all(join_heads(results[3]), "seq", split_axis=1, concat_axis=2, tiled=True),
    )
    every_sequence = lax.all_gather(attended, "tp", axis=0, tiled=True)
    grad_weight = lax.psum_scatter(
        jnp.einsum(
            "str,stc->rc", every_sequence, upstream, preferred_element_type=jnp.float32
        ).astype(jnp.bfloat16),
        "seq",
        scatter_dimension=0,
        tiled=True,
    ).astype(jnp.float32)
    return (attended, query_grad, key_grad, value_grad, grad_weight)


def solution(mesh):
    in_specs = (
        P("tp", "seq", None),
        P("tp", "seq", None),
        P("tp", "seq", None),
        P(None, "seq", "tp"),
        P(None, "tp"),
        P(),
    )
    out_specs = (
        P("tp", "seq", None),
        P("tp", "seq", None),
        P("tp", "seq", None),
        P("tp", "seq", None),
        P("seq", "tp"),
    )
    return jax.shard_map(
        on_device, mesh=mesh, in_specs=in_specs, out_specs=out_specs, check_vma=False
    )
```

profile of v0, /device:TPU:32, one launch (start us, length us, event | category | flops | bytes accessed | tf_op | source)
XLA Modules:
  0.0 871.2 jit_solution(8195947875667358401)
XLA Ops:
  8.4 8.9 %convolution_convert_fusion = bf16[8,128,4096]{2,1,0:T(8,128)(2,1)} fusion(bf16[8,128,512]{2,1,0:T(8,128)(2,1)S(1)} %copy-done, bf16[4096,512]{1,0:T(8,128)(2,1)} %param.10), kind=kOutput, calls=%fused_computation.6 | convolution fusion | flops 4299161600 | bytes 13631488 | tf_op jit(solution)/shard_map/stc,dc->std/dot_general | solution.py:88
  17.3 5.0 copy.81
  22.9 23.4 %reduce.1 = bf16[4096,128]{1,0:T(8,128)(2,1)} reduce(bf16[4096,1,128]{2,1,0:T(2,128)(2,1)S(1)} %bitcast.130, bf16[]{:T(256)} %broadcast.81), dimensions={1}, to_apply=%bitcast.71.reduce_sub_computation | reduce | bytes 2097154
  46.3 2.1 reshape.139
  48.4 11.9 %all-to-all-start.2 = ((bf16[32,2,8192]{2,1,0:T(2,128)(2,1)}), bf16[32,2,8192]{2,1,0:T(2,128)(2,1)}, u32[]{:S(2)}, u32[]{:S(2)}) async-start(bf16[32,2,8192]{2,1,0:T(2,128)(2,1)} %reshape.139), calls=%async_computation.2 | async-start | bytes 2097152 | tf_op jit(solution)/shard_map/all_to_all | solution.py:72
  60.3 5.0 copy.76
  65.3 23.4 %reduce.2 = bf16[4096,128]{1,0:T(8,128)(2,1)} reduce(bf16[4096,1,128]{2,1,0:T(2,128)(2,1)S(1)} %bitcast.136, bf16[]{:T(256)} %broadcast.81), dimensions={1}, to_apply=%bitcast.73.reduce_sub_computation | reduce | bytes 2097154
  88.7 2.1 reshape.141
  90.8 9.9 %all-to-all-start = ((bf16[32,2,8192]{2,1,0:T(2,128)(2,1)}), bf16[32,2,8192]{2,1,0:T(2,128)(2,1)}, u32[]{:S(2)}, u32[]{:S(2)}) async-start(bf16[32,2,8192]{2,1,0:T(2,128)(2,1)} %reshape.141), calls=%async_computation | async-start | bytes 2097152 | tf_op jit(solution)/shard_map/all_to_all | solution.py:71
  100.7 5.0 copy.79
  105.8 23.4 %reduce.3 = bf16[4096,128]{1,0:T(8,128)(2,1)} reduce(bf16[4096,1,128]{2,1,0:T(2,128)(2,1)S(1)} %bitcast.137, bf16[]{:T(256)} %broadcast.81), dimensions={1}, to_apply=%bitcast.75.reduce_sub_computation | reduce | bytes 2097154
  129.1 2.1 reshape.143
  131.4 10.1 %all-to-all-start.1 = ((bf16[32,2,8192]{2,1,0:T(2,128)(2,1)}), bf16[32,2,8192]{2,1,0:T(2,128)(2,1)}, u32[]{:S(2)}, u32[]{:S(2)}) async-start(bf16[32,2,8192]{2,1,0:T(2,128)(2,1)} %reshape.143), calls=%async_computation.1 | async-start | bytes 2097152 | tf_op jit(solution)/shard_map/all_to_all | solution.py:70
  141.5 84.0 %reduce-scatter.3.cloned.1.call-done = bf16[1,128,4096]{2,1,0:T(8,128)(2,1)} async-done(((bf16[8,128,4096]{2,1,0:T(8,128)(2,1)}), bf16[1,128,4096]{2,1,0:T(8,128)(2,1)}) %reduce-scatter.3.cloned.1.call-update) | async-done | bytes 1048592 | tf_op jit(solution)/shard_map/reduce_scatter | solution.py:87
  225.5 5.0 copy.85
  230.6 23.4 %reduce = bf16[4096,128]{1,0:T(8,128)(2,1)} reduce(bf16[4096,1,128]{2,1,0:T(2,128)(2,1)S(1)} %bitcast.132, bf16[]{:T(256)} %broadcast.81), dimensions={1}, to_apply=%bitcast.79.reduce_sub_computation | reduce | bytes 2097154
  253.9 2.1 reshape.147
  256.1 9.8 %all-to-all-start.4 = ((bf16[32,2,8192]{2,1,0:T(2,128)(2,1)}), bf16[32,2,8192]{2,1,0:T(2,128)(2,1)}, u32[]{:S(2)}, u32[]{:S(2)}) async-start(bf16[32,2,8192]{2,1,0:T(2,128)(2,1)} %reshape.147), calls=%async_computation.5 | async-start | bytes 2097152 | tf_op jit(solution)/shard_map/all_to_all | solution.py:95
  266.2 4.3 reshape.140
  271.6 1.6 copy.82
  273.2 5.8 reshape.142
  279.0 2.7 copy.101
  281.7 1.6 copy.77
  283.3 3.0 gather_fusion.1
  286.3 3.0 gather_fusion
  289.4 4.3 reshape.144
  294.8 1.6 copy.80
  296.4 3.8 fusion.24
  300.2 2.0 copy-done.2
  302.2 2.9 fusion.21
  305.0 5.8 reshape.148
  310.8 1.7 copy.105
  312.5 1.3 copy.86
  313.9 12.7 %multiply_reduce_fusion = (f32[64,64]{1,0:T(8,128)S(1)}, bf16[64,64,128]{2,1,0:T(8,128)(2,1)S(1)}) fusion(bf16[64,64,128]{2,1,0:T(8,128)(2,1)} %bitcast.156, bf16[64,256,128]{2,1,0:T(8,128)(2,1)} %bitcast.149, f32[64,64]{1,0:T(8,128)S(1)} %get-tuple-element.65, f32[64,256,64]{1,2,0:T(8,128)} %copy-done.2), kind=kOutput, calls=%fused_computation.14 | convolution fusion | flops 276300032 | bytes 10518528 | tf_op jit(solution)/shard_map/while/body/eval_jaxpr/qij,qjd->qid/dot_general | solution.py:26
  326.6 17.5 %copy.116 = bf16[1,4096,128]{2,0,1:T(2,128)(2,1)} copy(bf16[1,4096,128]{2,1,0:T(8,128)(2,1)S(1)} %bitcast.155) | data formatting | bytes 2097152 | tf_op jit(solution)/shard_map/reshape;transpose;reshape | solution.py:84
  344.0 23.4 %reduce.4 = bf16[4096,128]{1,0:T(8,128)(2,1)S(1)} reduce(bf16[4096,1,128]{2,1,0:T(2,128)(2,1)} %bitcast.133, bf16[]{:T(256)} %broadcast.81), dimensions={1}, to_apply=%bitcast.113.reduce_sub_computation | reduce | bytes 2097154
  368.6 40.3 %all_to_all.132 = bf16[32,2,8192]{2,1,0:T(2,128)(2,1)S(1)} all-to-all(bf16[32,2,8192]{2,1,0:T(2,128)(2,1)} %reshape.145), channel_id=1, replica_groups=mesh['seq'=32,'tp'=8] {'seq'}, dimensions={0} | all-to-all | bytes 2097152 | tf_op jit(solution)/shard_map/all_to_all | solution.py:109
  408.9 3.5 reshape.146
  412.3 1.7 copy.104
  415.4 2.3 copy.96
  417.7 7.5 multiply_convert_fusion
  425.2 158.5 %all-gather.2.cloned.1.call-done = bf16[8,128,4096]{2,1,0:T(8,128)(2,1)} async-done(((bf16[1,128,4096]{2,1,0:T(8,128)(2,1)}), bf16[8,128,4096]{2,1,0:T(8,128)(2,1)}) %all-gather.2.cloned.1.call-update) | async-done | bytes 8388624 | tf_op jit(solution)/shard_map/all_gather | solution.py:114
  583.7 9.7 %bitcast_convert_fusion = bf16[4096,512]{1,0:T(8,128)(2,1)} fusion(bf16[8,128,4096]{2,1,0:T(8,128)(2,1)} %all-gather.2.cloned.1.call-done, bf16[8,128,512]{2,1,0:T(8,128)(2,1)S(1)} %copy-done), kind=kOutput, calls=%fused_computation.5 | convolution fusion | flops 4297064448 | bytes 13631488 | tf_op jit(solution)/shard_map/str,stc->rc/dot_general | solution.py:116
  593.5 3.7 convolution_convert_fusion.1
  597.2 17.0 %copy.115 = bf16[1,4096,128]{2,0,1:T(2,128)(2,1)} copy(bf16[1,4096,128]{2,1,0:T(8,128)(2,1)S(1)} %bitcast.138) | data formatting | bytes 2097152 | tf_op jit(solution)/shard_map/reshape;transpose;reshape | solution.py:84
  614.2 23.5 %reduce.5 = bf16[4096,128]{1,0:T(8,128)(2,1)S(1)} reduce(bf16[4096,1,128]{2,1,0:T(2,128)(2,1)} %bitcast.134, bf16[]{:T(256)} %broadcast.81), dimensions={1}, to_apply=%bitcast.112.reduce_sub_computation | reduce | bytes 2097154
  638.8 10.2 %all-to-all-start.5 = ((bf16[32,2,8192]{2,1,0:T(2,128)(2,1)}), bf16[32,2,8192]{2,1,0:T(2,128)(2,1)}, u32[]{:S(2)}, u32[]{:S(2)}) async-start(bf16[32,2,8192]{2,1,0:T(2,128)(2,1)} %reshape.149), calls=%async_computation.6 | async-start | bytes 2097152 | tf_op jit(solution)/shard_map/all_to_all | solution.py:110
  649.2 6.1 fusion.25
  655.5 26.3 %scatter_fusion = f32[64,64,128]{2,1,0:T(8,128)S(1)} fusion(f32[64,64,128]{2,1,0:T(8,128)S(1)} %broadcast.50.clone, s32[256]{0:T(256)S(1)} %bitcast.159, f32[256,64,128]{2,1,0:T(8,128)} %bitcast.116), kind=kCustom, calls=%fused_computation.2 | custom fusion | flops 2097152 | bytes 25166848 | tf_op jit(solution)/shard_map/while/body/eval_jaxpr/scatter-add | solution.py:56
  682.0 16.7 %copy.114 = bf16[1,4096,128]{2,0,1:T(2,128)(2,1)S(1)} copy(bf16[1,4096,128]{2,1,0:T(8,128)(2,1)S(1)} %bitcast.139) | data formatting | bytes 2097152 | tf_op jit(solution)/shard_map/reshape;transpose;reshape | solution.py:84
  698.8 22.4 %reduce.6 = bf16[4096,128]{1,0:T(8,128)(2,1)S(1)} reduce(bf16[4096,1,128]{2,1,0:T(2,128)(2,1)S(1)} %bitcast.135, bf16[]{:T(256)} %broadcast.81), dimensions={1}, to_apply=%bitcast.111.reduce_sub_computation | reduce | bytes 2097154
  722.3 10.3 %all-to-all-start.6 = ((bf16[32,2,8192]{2,1,0:T(2,128)(2,1)}), bf16[32,2,8192]{2,1,0:T(2,128)(2,1)}, u32[]{:S(2)}, u32[]{:S(2)}) async-start(bf16[32,2,8192]{2,1,0:T(2,128)(2,1)} %reshape.151), calls=%async_computation.7 | async-start | bytes 2097152 | tf_op jit(solution)/shard_map/all_to_all | solution.py:111
  732.6 14.2 %fusion.10 = f32[64,256,128]{2,1,0:T(8,128)} fusion(bf16[64,64,128]{2,1,0:T(8,128)(2,1)S(1)} %bitcast.158, f32[64,64]{1,0:T(8,128)S(1)} %get-tuple-element.65, f32[64,256,64]{1,2,0:T(8,128)} %copy-done.2), kind=kOutput, calls=%fused_computation.24 | convolution fusion | flops 273682688 | bytes 13647872 | tf_op jit(solution)/shard_map/while/body/eval_jaxpr/qij,qid->qjd/dot_general | solution.py:50
  747.0 26.2 %scatter_fusion.1 = f32[64,64,128]{2,1,0:T(8,128)S(1)} fusion(f32[64,64,128]{2,1,0:T(8,128)S(1)} %broadcast.50.clone.1, s32[256]{0:T(256)S(1)} %bitcast.160, f32[256,64,128]{2,1,0:T(8,128)} %bitcast.129), kind=kCustom, calls=%fused_computation.3 | custom fusion | flops 2097152 | bytes 25166848 | tf_op jit(solution)/shard_map/while/body/eval_jaxpr/scatter-add | solution.py:62
  773.5 16.7 %copy.113 = bf16[1,4096,128]{2,0,1:T(2,128)(2,1)S(1)} copy(bf16[1,4096,128]{2,1,0:T(8,128)(2,1)S(1)} %bitcast.140) | data formatting | bytes 2097152 | tf_op jit(solution)/shard_map/reshape;transpose;reshape | solution.py:84
  790.2 22.4 %reduce.7 = bf16[4096,128]{1,0:T(8,128)(2,1)S(1)} reduce(bf16[4096,1,128]{2,1,0:T(2,128)(2,1)S(1)} %bitcast.131, bf16[]{:T(256)} %broadcast.81), dimensions={1}, to_apply=%bitcast.110.reduce_sub_computation | reduce | bytes 2097154
  813.7 9.9 %all-to-all-start.7 = ((bf16[32,2,8192]{2,1,0:T(2,128)(2,1)}), bf16[32,2,8192]{2,1,0:T(2,128)(2,1)}, u32[]{:S(2)}, u32[]{:S(2)}) async-start(bf16[32,2,8192]{2,1,0:T(2,128)(2,1)} %reshape.153), calls=%async_computation.8 | async-start | bytes 2097152 | tf_op jit(solution)/shard_map/all_to_all | solution.py:112
  823.6 4.3 reshape.150
  828.7 1.3 copy.97
  830.0 4.3 reshape.152
  836.5 17.7 %all-to-all-done.7 = bf16[32,2,8192]{2,1,0:T(2,128)(2,1)} async-done(((bf16[32,2,8192]{2,1,0:T(2,128)(2,1)}), bf16[32,2,8192]{2,1,0:T(2,128)(2,1)}, u32[]{:S(2)}, u32[]{:S(2)}) %all-to-all-start.7) | async-done | bytes 1048608 | tf_op jit(solution)/shard_map/all_to_all | solution.py:112
  854.1 4.4 reshape.154
  859.6 1.6 copy.93
  862.6 1.6 convert_element_type.51
  (48 shorter events, 16.6 us)
Async XLA Ops:
  7.2 1.2 copy-start
  7.2 218.3 %reduce-scatter.3.cloned.1.call-start = ((), (), s32[]{:S(2)}) async-start(), calls=%async_computation.10 | async-start | bytes 9437184 | tf_op jit(solution)/shard_map/reduce_scatter | solution.py:87
  48.4 42.4 %all-to-all-start.2 = ((bf16[32,2,8192]{2,1,0:T(2,128)(2,1)}), bf16[32,2,8192]{2,1,0:T(2,128)(2,1)}, u32[]{:S(2)}, u32[]{:S(2)}) async-start(bf16[32,2,8192]{2,1,0:T(2,128)(2,1)} %reshape.139), calls=%async_computation.2 | async-start | bytes 2097152 | tf_op jit(solution)/shard_map/all_to_all | solution.py:72
  90.8 40.5 %all-to-all-start = ((bf16[32,2,8192]{2,1,0:T(2,128)(2,1)}), bf16[32,2,8192]{2,1,0:T(2,128)(2,1)}, u32[]{:S(2)}, u32[]{:S(2)}) async-start(bf16[32,2,8192]{2,1,0:T(2,128)(2,1)} %reshape.141), calls=%async_computation | async-start | bytes 2097152 | tf_op jit(solution)/shard_map/all_to_all | solution.py:71
  131.4 124.7 %all-to-all-start.1 = ((bf16[32,2,8192]{2,1,0:T(2,128)(2,1)}), bf16[32,2,8192]{2,1,0:T(2,128)(2,1)}, u32[]{:S(2)}, u32[]{:S(2)}) async-start(bf16[32,2,8192]{2,1,0:T(2,128)(2,1)} %reshape.143), calls=%async_computation.1 | async-start | bytes 2097152 | tf_op jit(solution)/shard_map/all_to_all | solution.py:70
  230.5 35.4 %copy-start.4 = (s32[64,4]{0,1:T(4,128)S(1)}, s32[64,4]{0,1:T(4,128)}, u32[]{:S(2)}) copy-start(s32[64,4]{0,1:T(4,128)} %param.11) | copy-start | bytes 3076
  256.1 49.0 %all-to-all-start.4 = ((bf16[32,2,8192]{2,1,0:T(2,128)(2,1)}), bf16[32,2,8192]{2,1,0:T(2,128)(2,1)}, u32[]{:S(2)}, u32[]{:S(2)}) async-start(bf16[32,2,8192]{2,1,0:T(2,128)(2,1)} %reshape.147), calls=%async_computation.5 | async-start | bytes 2097152 | tf_op jit(solution)/shard_map/all_to_all | solution.py:95
  265.9 317.8 %all-gather.2.cloned.1.call-start = ((), (), s32[]{:S(2)}) async-start(), calls=%async_computation.11 | async-start | bytes 9437184 | tf_op jit(solution)/shard_map/all_gather | solution.py:114
  300.2 2.0 copy-start.2
  417.7 444.9 %reduce-scatter.5.cloned.1.call-start = ((), (), s32[]{:S(2)}) async-start(), calls=%async_computation.12 | async-start | bytes 4325376 | tf_op jit(solution)/shard_map/reduce_scatter | solution.py:115
  638.8 83.5 %all-to-all-start.5 = ((bf16[32,2,8192]{2,1,0:T(2,128)(2,1)}), bf16[32,2,8192]{2,1,0:T(2,128)(2,1)}, u32[]{:S(2)}, u32[]{:S(2)}) async-start(bf16[32,2,8192]{2,1,0:T(2,128)(2,1)} %reshape.149), calls=%async_computation.6 | async-start | bytes 2097152 | tf_op jit(solution)/shard_map/all_to_all | solution.py:110
  721.2 11.4 %copy-start.3 = (bf16[1,32,128,128]{3,2,1,0:T(8,128)(2,1)S(1)}, bf16[1,32,128,128]{3,2,1,0:T(8,128)(2,1)}, u32[]{:S(2)}) copy-start(bf16[1,32,128,128]{3,2,1,0:T(8,128)(2,1)} %copy.86) | copy-start | bytes 3145732
  722.3 91.4 %all-to-all-start.6 = ((bf16[32,2,8192]{2,1,0:T(2,128)(2,1)}), bf16[32,2,8192]{2,1,0:T(2,128)(2,1)}, u32[]{:S(2)}, u32[]{:S(2)}) async-start(bf16[32,2,8192]{2,1,0:T(2,128)(2,1)} %reshape.151), calls=%async_computation.7 | async-start | bytes 2097152 | tf_op jit(solution)/shard_map/all_to_all | solution.py:111
  813.7 40.4 %all-to-all-start.7 = ((bf16[32,2,8192]{2,1,0:T(2,128)(2,1)}), bf16[32,2,8192]{2,1,0:T(2,128)(2,1)}, u32[]{:S(2)}, u32[]{:S(2)}) async-start(bf16[32,2,8192]{2,1,0:T(2,128)(2,1)} %reshape.153), calls=%async_computation.8 | async-start | bytes 2097152 | tf_op jit(solution)/shard_map/all_to_all | solution.py:112
  854.1 10.1 %copy-start.1 = (bf16[8,128,512]{2,1,0:T(8,128)(2,1)S(1)}, bf16[8,128,512]{2,1,0:T(8,128)(2,1)}, u32[]{:S(2)}) copy-start(bf16[8,128,512]{2,1,0:T(8,128)(2,1)} %param.9) | copy-start | bytes 3145732
Sparse Core Ops, SparseCore 0:
  17.5 208.0 reduce-scatter.2
  417.8 165.8 all-gather.1
  593.6 137.1 reduce-scatter.4
where the time goes:
time: 881 us; the launch traced here: 871 us
  waiting for transfers between devices  260 us (30%)
  other arithmetic  243 us (28%)
  local copies, waits for them, and re-layouts  175 us (20%)
  starting transfers between devices  72.2 us (8%)
  matrix products  66.5 us (8%)
  blocking collectives  40.3 us (5%)
  between operations  14.6 us (2%)
    unnamed x8, other arithmetic  185 us
    all_gather x1, waiting for transfers between devices, on_device(): every_sequence = lax.all_gather(attended, 'tp', axis=0, tiled=True)  159 us
    unnamed x43, local copies, waits for them, and re-layouts  84.4 us
    reduce_scatter x1, waiting for transfers between devices, on_device(): lax.psum_scatter(jnp.einsum('stc,dc->std', upstream, out_weight, preferre...  84 us
    another operation x4, local copies, waits for them, and re-layouts, join_heads(): return array.reshape(count_heads, length, HD).transpose(1, 0, 2).reshape(...  68 us
    all_to_all x1, blocking collectives, on_device(): lax.all_to_all(join_heads(results[0]), 'seq', split_axis=1, concat_axis=2...  40.3 us
    scatter-add x1, other arithmetic, backward_head(): key_grad = jnp.zeros((block_count, BLK, HD), jnp.float32).at[flat_list].a...  26.3 us
    scatter-add x1, other arithmetic, backward_head(): value_grad = jnp.zeros((block_count, BLK, HD), jnp.float32).at[flat_list]...  26.2 us
  transfers between devices with their start and end apart: 10, of which 4 were waited for; matrix products, arithmetic and copies ran while one was open for 45% of the time, Pallas kernels for 0%

commit v1 on v0

--- a/solution.py
+++ b/solution.py
@@ -111,7 +111,9 @@
         lax.all_to_all(join_heads(results[2]), "seq", split_axis=1, concat_axis=2, tiled=True),
         lax.all_to_all(join_heads(results[3]), "seq", split_axis=1, concat_axis=2, tiled=True),
     )
-    every_sequence = lax.all_gather(attended, "tp", axis=0, tiled=True)
+    every_sequence = jnp.concatenate(
+        lax.all_to_all(jnp.stack([attended] * lax.axis_size("tp")), "tp", 0, 0), axis=0
+    )
     grad_weight = lax.psum_scatter(
         jnp.einsum(
             "str,stc->rc", every_sequence, upstream, preferred_element_type=jnp.float32

time: 881 us -> 813 us (0.923)
  waiting for transfers between devices: 260 us -> 187 us
    all_gather x1 -> x0, waiting for transfers between devices: 159 us -> none  [on_device(): every_sequence = lax.all_gather(attended, 'tp', axis=0, tiled=True)]
    all_to_all x0 -> x1, waiting for transfers between devices: none -> 86.5 us  [on_device(): lax.all_to_all(jnp.stack([attended] * lax.axis_size('tp')), 'tp', 0, 0)]
    unnamed x43 -> x47, local copies, waits for them, and re-layouts: 84.4 us -> 85.4 us
  transfers between devices with their start and end apart: 10 -> 10, of which waited for: 4 -> 4; matrix products, arithmetic and copies ran while one was open for 45% -> 49% of each run, Pallas kernels for 0% -> 0%
where the time goes in v1:
time: 813 us; the launch traced here: 803 us
  other arithmetic  244 us (30%)
  waiting for transfers between devices  187 us (23%)
  local copies, waits for them, and re-layouts  180 us (22%)
  starting transfers between devices  71.9 us (9%)
  matrix products  64.8 us (8%)
  blocking collectives  40.3 us (5%)
  between operations  14.9 us (2%)
    unnamed x8, other arithmetic  186 us
    all_to_all x1, waiting for transfers between devices, on_device(): lax.all_to_all(jnp.stack([attended] * lax.axis_size('tp')), 'tp', 0, 0)  86.5 us
    unnamed x47, local copies, waits for them, and re-layouts  85.4 us
    reduce_scatter x1, waiting for transfers between devices, on_device(): lax.psum_scatter(jnp.einsum('stc,dc->std', upstream, out_weight, preferre...  84 us
    another operation x4, local copies, waits for them, and re-layouts, join_heads(): return array.reshape(count_heads, length, HD).transpose(1, 0, 2).reshape(...  68 us
    all_to_all x1, blocking collectives, on_device(): lax.all_to_all(join_heads(results[0]), 'seq', split_axis=1, concat_axis=2...  40.3 us
    scatter-add x1, other arithmetic, backward_head(): key_grad = jnp.zeros((block_count, BLK, HD), jnp.float32).at[flat_list].a...  26.2 us
    scatter-add x1, other arithmetic, backward_head(): value_grad = jnp.zeros((block_count, BLK, HD), jnp.float32).at[flat_list]...  26.2 us
  transfers between devices with their start and end apart: 10, of which 4 were waited for; matrix products, arithmetic and copies ran while one was open for 49% of the time, Pallas kernels for 0%

profile of v1, /device:TPU:32, one launch (start us, length us, event | category | flops | bytes accessed | tf_op | source)
XLA Modules:
  0.0 802.8 jit_solution(13075344616487689444)
XLA Ops:
  8.4 8.9 %convolution_convert_fusion = bf16[8,128,4096]{2,1,0:T(8,128)(2,1)} fusion(bf16[8,128,512]{2,1,0:T(8,128)(2,1)S(1)} %copy-done, bf16[4096,512]{1,0:T(8,128)(2,1)} %param.10), kind=kOutput, calls=%fused_computation.8 | convolution fusion | flops 4299161600 | bytes 13631488 | tf_op jit(solution)/shard_map/stc,dc->std/dot_general | solution.py:88
  17.3 5.0 copy.80
  22.9 23.4 %reduce.1 = bf16[4096,128]{1,0:T(8,128)(2,1)} reduce(bf16[4096,1,128]{2,1,0:T(2,128)(2,1)S(1)} %bitcast.137, bf16[]{:T(256)} %broadcast.83), dimensions={1}, to_apply=%bitcast.77.reduce_sub_computation | reduce | bytes 2097154
  46.3 2.1 reshape.148
  48.4 11.9 %all-to-all-start.2 = ((bf16[32,2,8192]{2,1,0:T(2,128)(2,1)}), bf16[32,2,8192]{2,1,0:T(2,128)(2,1)}, u32[]{:S(2)}, u32[]{:S(2)}) async-start(bf16[32,2,8192]{2,1,0:T(2,128)(2,1)} %reshape.148), calls=%async_computation.2 | async-start | bytes 2097152 | tf_op jit(solution)/shard_map/all_to_all | solution.py:72
  60.3 5.0 copy.75
  65.3 23.4 %reduce.2 = bf16[4096,128]{1,0:T(8,128)(2,1)} reduce(bf16[4096,1,128]{2,1,0:T(2,128)(2,1)S(1)} %bitcast.143, bf16[]{:T(256)} %broadcast.83), dimensions={1}, to_apply=%bitcast.79.reduce_sub_computation | reduce | bytes 2097154
  88.7 2.1 reshape.150
  90.8 9.9 %all-to-all-start = ((bf16[32,2,8192]{2,1,0:T(2,128)(2,1)}), bf16[32,2,8192]{2,1,0:T(2,128)(2,1)}, u32[]{:S(2)}, u32[]{:S(2)}) async-start(bf16[32,2,8192]{2,1,0:T(2,128)(2,1)} %reshape.150), calls=%async_computation | async-start | bytes 2097152 | tf_op jit(solution)/shard_map/all_to_all | solution.py:71
  100.7 5.0 copy.78
  105.8 23.4 %reduce.3 = bf16[4096,128]{1,0:T(8,128)(2,1)} reduce(bf16[4096,1,128]{2,1,0:T(2,128)(2,1)S(1)} %bitcast.144, bf16[]{:T(256)} %broadcast.83), dimensions={1}, to_apply=%bitcast.81.reduce_sub_computation | reduce | bytes 2097154
  129.1 2.1 reshape.152
  131.4 10.1 %all-to-all-start.1 = ((bf16[32,2,8192]{2,1,0:T(2,128)(2,1)}), bf16[32,2,8192]{2,1,0:T(2,128)(2,1)}, u32[]{:S(2)}, u32[]{:S(2)}) async-start(bf16[32,2,8192]{2,1,0:T(2,128)(2,1)} %reshape.152), calls=%async_computation.1 | async-start | bytes 2097152 | tf_op jit(solution)/shard_map/all_to_all | solution.py:70
  141.5 84.0 %reduce-scatter.3.cloned.1.call-done = bf16[1,128,4096]{2,1,0:T(8,128)(2,1)} async-done(((bf16[8,128,4096]{2,1,0:T(8,128)(2,1)}), bf16[1,128,4096]{2,1,0:T(8,128)(2,1)}) %reduce-scatter.3.cloned.1.call-update) | async-done | bytes 1048592 | tf_op jit(solution)/shard_map/reduce_scatter | solution.py:87
  225.5 5.0 copy.84
  230.6 23.4 %reduce = bf16[4096,128]{1,0:T(8,128)(2,1)} reduce(bf16[4096,1,128]{2,1,0:T(2,128)(2,1)S(1)} %bitcast.139, bf16[]{:T(256)} %broadcast.83), dimensions={1}, to_apply=%bitcast.85.reduce_sub_computation | reduce | bytes 2097154
  253.9 2.1 reshape.156
  256.1 9.8 %all-to-all-start.4 = ((bf16[32,2,8192]{2,1,0:T(2,128)(2,1)}), bf16[32,2,8192]{2,1,0:T(2,128)(2,1)}, u32[]{:S(2)}, u32[]{:S(2)}) async-start(bf16[32,2,8192]{2,1,0:T(2,128)(2,1)} %reshape.156), calls=%async_computation.5 | async-start | bytes 2097152 | tf_op jit(solution)/shard_map/all_to_all | solution.py:95
  266.1 4.3 reshape.149
  271.5 1.6 copy.81
  273.2 5.8 reshape.151
  279.0 2.7 copy.98
  281.6 1.6 copy.76
  283.3 3.1 gather_fusion.1
  286.3 3.1 gather_fusion
  289.4 4.3 reshape.153
  294.8 1.6 copy.79
  296.4 3.8 fusion.28
  300.2 1.9 copy-done.2
  302.1 2.8 fusion.25
  305.0 5.8 reshape.157
  310.7 1.7 copy.102
  313.8 12.7 %multiply_reduce_fusion = (f32[64,64]{1,0:T(8,128)S(1)}, bf16[64,64,128]{2,1,0:T(8,128)(2,1)S(1)}) fusion(bf16[64,64,128]{2,1,0:T(8,128)(2,1)} %bitcast.162, bf16[64,256,128]{2,1,0:T(8,128)(2,1)} %bitcast.156, f32[64,64]{1,0:T(8,128)S(1)} %get-tuple-element.55, f32[64,256,64]{1,2,0:T(8,128)} %copy-done.2), kind=kOutput, calls=%fused_computation.16 | convolution fusion | flops 276300032 | bytes 10518528 | tf_op jit(solution)/shard_map/while/body/eval_jaxpr/qij,qjd->qid/dot_general | solution.py:26
  326.5 17.5 %copy.113 = bf16[1,4096,128]{2,0,1:T(2,128)(2,1)} copy(bf16[1,4096,128]{2,1,0:T(8,128)(2,1)S(1)} %bitcast.161) | data formatting | bytes 2097152 | tf_op jit(solution)/shard_map/reshape;transpose;reshape | solution.py:84
  343.9 23.4 %reduce.4 = bf16[4096,128]{1,0:T(8,128)(2,1)S(1)} reduce(bf16[4096,1,128]{2,1,0:T(2,128)(2,1)} %bitcast.140, bf16[]{:T(256)} %broadcast.83), dimensions={1}, to_apply=%bitcast.118.reduce_sub_computation | reduce | bytes 2097154
  368.5 40.3 %all_to_all.137 = bf16[32,2,8192]{2,1,0:T(2,128)(2,1)S(1)} all-to-all(bf16[32,2,8192]{2,1,0:T(2,128)(2,1)} %reshape.154), channel_id=1, replica_groups=mesh['seq'=32,'tp'=8] {'seq'}, dimensions={0} | all-to-all | bytes 2097152 | tf_op jit(solution)/shard_map/all_to_all | solution.py:109
  408.8 3.5 reshape.155
  412.2 2.7 copy.101
  414.9 1.6 copy.83
  416.5 4.3 stack.5
  420.8 5.0 all-to-all-start.8
  425.9 7.4 multiply_convert_fusion
  433.3 86.5 %all-to-all-done.8 = bf16[8,1,128,4096]{2,3,1,0:T(8,128)(2,1)} async-done(((bf16[8,1,128,4096]{2,3,1,0:T(8,128)(2,1)}), bf16[8,1,128,4096]{2,3,1,0:T(8,128)(2,1)}, u32[]{:S(2)}, u32[]{:S(2)}) %all-to-all-start.8) | async-done | bytes 8388640 | tf_op jit(solution)/shard_map/all_to_all | solution.py:115
  519.8 8.2 %bitcast_convert_fusion = bf16[4096,512]{1,0:T(8,128)(2,1)} fusion(bf16[8,128,512]{2,1,0:T(8,128)(2,1)S(1)} %copy-done, bf16[8,1,128,4096]{2,3,1,0:T(8,128)(2,1)} %all-to-all-done.8), kind=kOutput, calls=%fused_computation.5 | convolution fusion | flops 4297064448 | bytes 13631488 | tf_op jit(solution)/shard_map/str,stc->rc/dot_general | solution.py:118
  528.0 3.7 convolution_convert_fusion.1
  531.7 17.0 %copy.112 = bf16[1,4096,128]{2,0,1:T(2,128)(2,1)} copy(bf16[1,4096,128]{2,1,0:T(8,128)(2,1)S(1)} %bitcast.145) | data formatting | bytes 2097152 | tf_op jit(solution)/shard_map/reshape;transpose;reshape | solution.py:84
  548.7 23.5 %reduce.5 = bf16[4096,128]{1,0:T(8,128)(2,1)S(1)} reduce(bf16[4096,1,128]{2,1,0:T(2,128)(2,1)} %bitcast.141, bf16[]{:T(256)} %broadcast.83), dimensions={1}, to_apply=%bitcast.117.reduce_sub_computation | reduce | bytes 2097154
  573.3 4.9 all-to-all-start.5
  578.4 6.1 fusion.29
  584.8 26.2 %scatter_fusion = f32[64,64,128]{2,1,0:T(8,128)S(1)} fusion(f32[64,64,128]{2,1,0:T(8,128)S(1)} %broadcast.52.clone, s32[256]{0:T(256)S(1)} %bitcast.165, f32[256,64,128]{2,1,0:T(8,128)} %bitcast.121), kind=kCustom, calls=%fused_computation.2 | custom fusion | flops 2097152 | bytes 25166848 | tf_op jit(solution)/shard_map/while/body/eval_jaxpr/scatter-add | solution.py:56
  611.2 16.7 %copy.111 = bf16[1,4096,128]{2,0,1:T(2,128)(2,1)S(1)} copy(bf16[1,4096,128]{2,1,0:T(8,128)(2,1)S(1)} %bitcast.146) | data formatting | bytes 2097152 | tf_op jit(solution)/shard_map/reshape;transpose;reshape | solution.py:84
  628.0 22.4 %reduce.6 = bf16[4096,128]{1,0:T(8,128)(2,1)S(1)} reduce(bf16[4096,1,128]{2,1,0:T(2,128)(2,1)S(1)} %bitcast.142, bf16[]{:T(256)} %broadcast.83), dimensions={1}, to_apply=%bitcast.116.reduce_sub_computation | reduce | bytes 2097154
  651.5 10.3 %all-to-all-start.6 = ((bf16[32,2,8192]{2,1,0:T(2,128)(2,1)}), bf16[32,2,8192]{2,1,0:T(2,128)(2,1)}, u32[]{:S(2)}, u32[]{:S(2)}) async-start(bf16[32,2,8192]{2,1,0:T(2,128)(2,1)} %reshape.160), calls=%async_computation.7 | async-start | bytes 2097152 | tf_op jit(solution)/shard_map/all_to_all | solution.py:111
  661.8 14.1 %fusion.14 = f32[64,256,128]{2,1,0:T(8,128)} fusion(bf16[64,64,128]{2,1,0:T(8,128)(2,1)S(1)} %bitcast.164, f32[64,64]{1,0:T(8,128)S(1)} %get-tuple-element.55, f32[64,256,64]{1,2,0:T(8,128)} %copy-done.2), kind=kOutput, calls=%fused_computation.26 | convolution fusion | flops 273682688 | bytes 13647872 | tf_op jit(solution)/shard_map/while/body/eval_jaxpr/qij,qid->qjd/dot_general | solution.py:50
  676.2 26.2 %scatter_fusion.1 = f32[64,64,128]{2,1,0:T(8,128)S(1)} fusion(f32[64,64,128]{2,1,0:T(8,128)S(1)} %broadcast.52.clone.1, s32[256]{0:T(256)S(1)} %bitcast.166, f32[256,64,128]{2,1,0:T(8,128)} %bitcast.136), kind=kCustom, calls=%fused_computation.3 | custom fusion | flops 2097152 | bytes 25166848 | tf_op jit(solution)/shard_map/while/body/eval_jaxpr/scatter-add | solution.py:62
  702.6 16.7 %copy.110 = bf16[1,4096,128]{2,0,1:T(2,128)(2,1)S(1)} copy(bf16[1,4096,128]{2,1,0:T(8,128)(2,1)S(1)} %bitcast.147) | data formatting | bytes 2097152 | tf_op jit(solution)/shard_map/reshape;transpose;reshape | solution.py:84
  719.4 23.5 %reduce.7 = bf16[4096,128]{1,0:T(8,128)(2,1)} reduce(bf16[4096,1,128]{2,1,0:T(2,128)(2,1)S(1)} %bitcast.138, bf16[]{:T(256)} %broadcast.83), dimensions={1}, to_apply=%bitcast.115.reduce_sub_computation | reduce | bytes 2097154
  742.8 2.2 reshape.162
  745.0 9.9 %all-to-all-start.7 = ((bf16[32,2,8192]{2,1,0:T(2,128)(2,1)}), bf16[32,2,8192]{2,1,0:T(2,128)(2,1)}, u32[]{:S(2)}, u32[]{:S(2)}) async-start(bf16[32,2,8192]{2,1,0:T(2,128)(2,1)} %reshape.162), calls=%async_computation.8 | async-start | bytes 2097152 | tf_op jit(solution)/shard_map/all_to_all | solution.py:112
  756.2 4.3 reshape.159
  762.6 4.3 reshape.161
  769.1 16.3 %all-to-all-done.7 = bf16[32,2,8192]{2,1,0:T(2,128)(2,1)} async-done(((bf16[32,2,8192]{2,1,0:T(2,128)(2,1)}), bf16[32,2,8192]{2,1,0:T(2,128)(2,1)}, u32[]{:S(2)}, u32[]{:S(2)}) %all-to-all-start.7) | async-done | bytes 1048608 | tf_op jit(solution)/shard_map/all_to_all | solution.py:112
  785.4 4.4 reshape.163
  793.9 1.6 convert_element_type.51
  (52 shorter events, 19.7 us)
Async XLA Ops:
  7.2 1.2 copy-start
  7.2 218.3 %reduce-scatter.3.cloned.1.call-start = ((), (), s32[]{:S(2)}) async-start(), calls=%async_computation.11 | async-start | bytes 9437184 | tf_op jit(solution)/shard_map/reduce_scatter | solution.py:87
  48.4 42.4 %all-to-all-start.2 = ((bf16[32,2,8192]{2,1,0:T(2,128)(2,1)}), bf16[32,2,8192]{2,1,0:T(2,128)(2,1)}, u32[]{:S(2)}, u32[]{:S(2)}) async-start(bf16[32,2,8192]{2,1,0:T(2,128)(2,1)} %reshape.148), calls=%async_computation.2 | async-start | bytes 2097152 | tf_op jit(solution)/shard_map/all_to_all | solution.py:72
  90.8 40.5 %all-to-all-start = ((bf16[32,2,8192]{2,1,0:T(2,128)(2,1)}), bf16[32,2,8192]{2,1,0:T(2,128)(2,1)}, u32[]{:S(2)}, u32[]{:S(2)}) async-start(bf16[32,2,8192]{2,1,0:T(2,128)(2,1)} %reshape.150), calls=%async_computation | async-start | bytes 2097152 | tf_op jit(solution)/shard_map/all_to_all | solution.py:71
  131.4 124.7 %all-to-all-start.1 = ((bf16[32,2,8192]{2,1,0:T(2,128)(2,1)}), bf16[32,2,8192]{2,1,0:T(2,128)(2,1)}, u32[]{:S(2)}, u32[]{:S(2)}) async-start(bf16[32,2,8192]{2,1,0:T(2,128)(2,1)} %reshape.152), calls=%async_computation.1 | async-start | bytes 2097152 | tf_op jit(solution)/shard_map/all_to_all | solution.py:70
  230.5 35.3 %copy-start.6 = (s32[64,4]{0,1:T(4,128)S(1)}, s32[64,4]{0,1:T(4,128)}, u32[]{:S(2)}) copy-start(s32[64,4]{0,1:T(4,128)} %param.11) | copy-start | bytes 3076
  256.1 48.9 %all-to-all-start.4 = ((bf16[32,2,8192]{2,1,0:T(2,128)(2,1)}), bf16[32,2,8192]{2,1,0:T(2,128)(2,1)}, u32[]{:S(2)}, u32[]{:S(2)}) async-start(bf16[32,2,8192]{2,1,0:T(2,128)(2,1)} %reshape.156), calls=%async_computation.5 | async-start | bytes 2097152 | tf_op jit(solution)/shard_map/all_to_all | solution.py:95
  300.2 1.9 copy-start.2
  416.5 4.3 copy-start.3
  420.8 98.9 %all-to-all-start.8 = ((bf16[8,1,128,4096]{2,3,1,0:T(8,128)(2,1)}), bf16[8,1,128,4096]{2,3,1,0:T(8,128)(2,1)}, u32[]{:S(2)}, u32[]{:S(2)}) async-start(bf16[8,1,128,4096]{2,3,1,0:T(8,128)(2,1)} %stack.5), calls=%async_computation.9 | async-start | bytes 16777216 | tf_op jit(solution)/shard_map/all_to_all | solution.py:115
  425.8 368.1 %reduce-scatter.5.cloned.1.call-start = ((), (), s32[]{:S(2)}) async-start(), calls=%async_computation.12 | async-start | bytes 4325376 | tf_op jit(solution)/shard_map/reduce_scatter | solution.py:117
  573.3 78.2 %all-to-all-start.5 = ((bf16[32,2,8192]{2,1,0:T(2,128)(2,1)}), bf16[32,2,8192]{2,1,0:T(2,128)(2,1)}, u32[]{:S(2)}, u32[]{:S(2)}) async-start(bf16[32,2,8192]{2,1,0:T(2,128)(2,1)} %reshape.158), calls=%async_computation.6 | async-start | bytes 2097152 | tf_op jit(solution)/shard_map/all_to_all | solution.py:110
  650.4 11.5 %copy-start.5 = (bf16[1,32,128,128]{3,2,1,0:T(8,128)(2,1)S(1)}, bf16[1,32,128,128]{3,2,1,0:T(8,128)(2,1)}, u32[]{:S(2)}) copy-start(bf16[1,32,128,128]{3,2,1,0:T(8,128)(2,1)} %copy.85) | copy-start | bytes 3145732
  651.5 93.5 %all-to-all-start.6 = ((bf16[32,2,8192]{2,1,0:T(2,128)(2,1)}), bf16[32,2,8192]{2,1,0:T(2,128)(2,1)}, u32[]{:S(2)}, u32[]{:S(2)}) async-start(bf16[32,2,8192]{2,1,0:T(2,128)(2,1)} %reshape.160), calls=%async_computation.7 | async-start | bytes 2097152 | tf_op jit(solution)/shard_map/all_to_all | solution.py:111
  719.3 35.5 %copy-start.4 = (bf16[1,128,32,128]{1,3,2,0:T(8,128)(2,1)S(1)}, bf16[1,128,32,128]{1,3,2,0:T(8,128)(2,1)}, u32[]{:S(2)}) copy-start(bf16[1,128,32,128]{1,3,2,0:T(8,128)(2,1)} %copy-done.3) | copy-start | bytes 3145732
  745.0 40.4 %all-to-all-start.7 = ((bf16[32,2,8192]{2,1,0:T(2,128)(2,1)}), bf16[32,2,8192]{2,1,0:T(2,128)(2,1)}, u32[]{:S(2)}, u32[]{:S(2)}) async-start(bf16[32,2,8192]{2,1,0:T(2,128)(2,1)} %reshape.162), calls=%async_computation.8 | async-start | bytes 2097152 | tf_op jit(solution)/shard_map/all_to_all | solution.py:112
  785.4 10.1 %copy-start.1 = (bf16[8,128,512]{2,1,0:T(8,128)(2,1)S(1)}, bf16[8,128,512]{2,1,0:T(8,128)(2,1)}, u32[]{:S(2)}) copy-start(bf16[8,128,512]{2,1,0:T(8,128)(2,1)} %param.9) | copy-start | bytes 3145732
Sparse Core Ops, SparseCore 0:
  17.5 208.0 reduce-scatter.2
  528.1 132.0 reduce-scatter.4
